TPU v7x, 128 devices: a whole 4x4x4 slice. The times are simulated.
128 devices in a mesh: dp: 8 (over x, core), fsdp: 16 (over y, z).
Axes of the slice: x: 4, y: 4, z: 4, core: 2. Of those that a mesh axis runs over, the one named last changes fastest.
Arguments:
- old_states: float32 [3, 2, 34816, 1792], P(None, None, ('dp', 'fsdp')), may hold values from -1.2 to 1.2, as said below
- old_bounds: int32 [8, 17], replicated, may hold values from 0 to 4096, as said below
- new_bounds: int32 [8, 17], replicated, may hold values from 0 to 4096, as said below
- failed: int32 [16], replicated, may hold values from 0 to 7, as said below
- tokens: bfloat16 [4096, 4096], P('fsdp'), may hold values from -6 to 6
- cotangent: bfloat16 [4096, 14336], P('fsdp', 'dp'), may hold values from -0.1875 to 0.1875
Outputs:
- new_states: float32 [3, 38912, 1792], P(None, ('dp', 'fsdp'))
- activations: bfloat16 [4096, 14336], P('fsdp', 'dp')
Inputs may be any that keep to these rules, and one draw needn't show every extreme that they name: Each row starts at 0, ends at 4096 and rises; old_bounds[g, f] is within 8 of f * 256, so each piece has 240 to 272 rows, and 272 is reached in every group. `new_bounds`: each row starts at 0 and ends at 4096; every entry is within 16 of the same entry of old_bounds, each piece has at most 304 rows, and 304 is reached in every group. `failed`: every group appears exactly 16 // 8 times. `old_states`: copy 0 of a failed device holds nothing of the states; the third state is positive.
All inputs are finite; a program needn't handle non-finite values.
Results may differ from a plain program's by a relative error of at most 0.018.
Values may be sent and summed in bfloat16 or wider, within the bound.
A program may use at most 192 MiB of HBM per device.

v0:
```python
import jax
import jax.numpy as jnp
from jax import lax
from jax.sharding import PartitionSpec as P

beta_one = 0.9
beta_two = 0.95
learn_rate = 0.01
decay_rate = 0.1
epsilon = 1e-08
correct_one = 1.0 - 0.9**8
correct_two = 1.0 - 0.95**8


def passed_along(value, axis, steps):
    count = lax.axis_size(axis)
    pairs = [(source, (source + steps) % count) for source in range(count)]
    return lax.ppermute(value, axis, pairs)


def extended_2(shard, sides, width):
    for axis, dim in sides:
        size, length = (lax.axis_size(axis), shard.shape[dim])
        up = [(i, (i + 1) % size) for i in range(size - 1)]
        down = [(j, i) for i, j in up]
        last = lax.slice_in_dim(shard, length - width, length, axis=dim)
        leading = lax.slice_in_dim(shard, 0, width, axis=dim)
        before = lax.ppermute(last, axis, up)
        after = lax.ppermute(leading, axis, down)
        shard = jnp.concatenate([before, shard, after], axis=dim)
    return shard


def pick_columns(tokens, bounds, row_count, capacity):
    flat_index = jnp.arange(row_count, dtype=jnp.int32)
    owner_ids = flat_index // capacity
    offsets = flat_index % capacity
    first_row = jnp.take(bounds, owner_ids)
    length = jnp.take(bounds, owner_ids + 1) - first_row
    target = jnp.minimum(first_row + offsets, tokens.shape[1] - 1)
    picked = jnp.take(tokens, target, axis=1)
    return jnp.where((offsets < length)[None, :], picked, jnp.zeros((), tokens.dtype))


def body(old_states, old_bounds, new_bounds, failed, tokens, cotangent):
    members = lax.axis_size("fsdp")
    my_group = lax.axis_index("dp")
    member_id = lax.axis_index("fsdp")
    lost_group = failed[member_id]
    rows_avg = tokens.shape[1] // members
    margin = rows_avg // 16
    cap_old = old_states.shape[2]
    cap_new = rows_avg + 3 * margin
    block_width = cotangent.shape[1]
    own_old = old_bounds[my_group]
    own_new = new_bounds[my_group]
    old_start = own_old[member_id]
    old_len = own_old[member_id + 1] - old_start
    new_start = own_new[member_id]
    new_len = own_new[member_id + 1] - new_start
    backup = old_states[:, 1]
    arrived = passed_along(backup.astype(jnp.bfloat16), "dp", 1).astype(backup.dtype)
    recovered = jnp.where(my_group == lost_group, arrived, old_states[:, 0])
    slot_old = jnp.arange(cap_old, dtype=jnp.int32)
    recovered = jnp.where(
        (slot_old < old_len)[None, :, None], recovered, jnp.zeros((), jnp.float32)
    )
    head_rows = recovered[:, :margin]
    tail_rows = lax.dynamic_slice_in_dim(recovered, old_len - margin, margin, 1)
    rim_rows = extended_2(
        jnp.concatenate([head_rows, tail_rows], 1).astype(jnp.bfloat16), (("fsdp", 1),), margin
    ).astype(jnp.float32)
    from_left = rim_rows[:, :margin]
    from_right = rim_rows[:, 3 * margin :]
    extended = jnp.zeros((3, margin + cap_old + margin + cap_new, block_width), jnp.float32)
    extended = lax.dynamic_update_slice_in_dim(extended, from_left, 0, 1)
    extended = lax.dynamic_update_slice_in_dim(extended, recovered, margin, 1)
    extended = lax.dynamic_update_slice_in_dim(extended, from_right, margin + old_len, 1)
    moved = lax.dynamic_slice_in_dim(extended, new_start - old_start + margin, cap_new, 1)
    slot_new = jnp.arange(cap_new, dtype=jnp.int32)
    moved = jnp.where((slot_new < new_len)[None, :, None], moved, jnp.zeros((), jnp.float32))
    block_rows = lax.all_gather(moved[0].astype(jnp.bfloat16), "fsdp", axis=0, tiled=True)
    picked = pick_columns(tokens, own_new, block_rows.shape[0], cap_new)
    hidden = jnp.dot(picked, block_rows, preferred_element_type=jnp.float32)
    activations = hidden.astype(jnp.bfloat16)
    picked = pick_columns(tokens, own_new, lax.axis_size("fsdp") * cap_new, cap_new)
    gradient = lax.psum_scatter(
        lax.dot_general(
            picked, cotangent, (((0,), (0,)), ((), ())), preferred_element_type=jnp.float32
        ).astype(jnp.bfloat16),
        "fsdp",
        scatter_dimension=0,
        tiled=True,
    ).astype(jnp.float32)
    weight = moved[0]
    moment_one = beta_one * moved[1] + (1.0 - beta_one) * gradient
    moment_two = beta_two * moved[2] + (1.0 - beta_two) * gradient * gradient
    update_dir = (
        moment_one / correct_one / (jnp.sqrt(moment_two / correct_two) + epsilon)
        + decay_rate * weight
    )
    new_weight = weight - learn_rate * update_dir
    return (jnp.stack([new_weight, moment_one, moment_two]), activations)


def solution(mesh):
    in_specs = (
        P(None, None, ("dp", "fsdp"), None),
        P(),
        P(),
        P(),
        P("fsdp", None),
        P("fsdp", "dp"),
    )
    out_specs = (P(None, ("dp", "fsdp"), None), P("fsdp", "dp"))
    return jax.shard_map(body, mesh=mesh, in_specs=in_specs, out_specs=out_specs, check_vma=False)
```

profile of v0, /device:TPU:1, one launch (start us, length us, event | category | flops | bytes accessed | tf_op | source)
XLA Modules:
  0.0 317.6 jit_solution(7382928010844779609)
XLA Ops:
  7.2 0.8 fusion.17
  8.0 0.7 fusion.20
  8.7 10.8 %compare_select_fusion = s32[4864]{0:T(1024)S(1)} fusion(s32[]{:T(128)} %bitcast.26, s32[]{:T(128)} %bitcast.25, s32[]{:T(128)} %bitcast.24, s32[]{:T(128)} %bitcast.23, s32[]{:T(128)} %bitcast.22, s32[]{:T(128)} %bitcast.21, s32[]{:T(128)} %bitcast.20, s32[]{:T(128)} %bitcast.19, s32[]{:T(128)} %bitcast.18, s32[]{:T(128)} %bitcast.17, s32[]{:T(128)} %bitcast.16, ...), kind=kLoop, calls=%fused_computation.31 | loop fusion | flops 272384 | bytes 19524 | tf_op jit(solution)/shard_map/jit(_take)/jit(_where)/select_n | solution.py:41
  19.5 10.8 %fusion.12 = (pred[4864]{0:T(1024)(128)(4,1)S(1)}, pred[4864]{0:T(1024)(128)(4,1)S(1)}) fusion(s32[]{:T(128)} %bitcast.26, s32[]{:T(128)} %bitcast.25, s32[]{:T(128)} %bitcast.24, s32[]{:T(128)} %bitcast.23, s32[]{:T(128)} %bitcast.22, s32[]{:T(128)} %bitcast.21, s32[]{:T(128)} %bitcast.20, s32[]{:T(128)} %bitcast.19, s32[]{:T(128)} %bitcast.18, ...), kind=kLoop, calls=%fused_computation.42 | loop fusion | flops 491264 | bytes 9796 | tf_op jit(solution)/shard_map/lt | solution.py:42
  30.4 3.3 %copy.10 = bf16[256,4096]{0,1:T(8,128)(2,1)S(1)} copy(bf16[256,4096]{1,0:T(8,128)(2,1)} %param.14) | data formatting | bytes 4194304 | tf_op args[4]
  33.7 14.4 %gather_fusion = bf16[4864,256]{1,0:T(8,128)(2,1)} fusion(bf16[256,4096]{0,1:T(8,128)(2,1)S(1)} %copy.10, s32[5120]{0:T(1024)S(1)} %pad_clamp_fusion), kind=kCustom, calls=%fused_computation.clone | custom fusion | bytes 5000192 | tf_op jit(solution)/shard_map/jit(_take)/gather | solution.py:41
  48.1 11.7 %convolution_convert_fusion = bf16[4864,1792]{1,0:T(8,128)(2,1)} fusion(bf16[256,1792]{1,0:T(8,128)(2,1)S(1)} %copy-done, bf16[4864,256]{1,0:T(8,128)(2,1)} %gather_fusion, pred[4864]{0:T(1024)(128)(4,1)S(1)} %get-tuple-element.35, pred[4864]{0:T(1024)(128)(4,1)S(1)} %get-tuple-element.34), kind=kOutput, calls=%fused_computation.1 | convolution fusion | flops 4473946112 | bytes 20850176 | tf_op jit(solution)/shard_map/dot_general | solution.py:88
  59.8 0.0 all-gather.2.cloned.1.call-start
  59.8 4.5 %fusion.2 = bf16[3,272,1792]{2,1,0:T(8,128)(2,1)} fusion(f32[3,2,272,1792]{3,2,1,0:T(8,128)} %param.10), kind=kLoop, calls=%fused_computation.9 | loop fusion | bytes 5849088 | tf_op jit(solution)/shard_map/convert_element_type | solution.py:62
  64.4 2.6 collective-permute-start
  67.0 0.6 dynamic_slice.29
  68.2 1.4 fusion.18
  70.9 28.2 %collective-permute-done = bf16[3,272,1792]{2,1,0:T(8,128)(2,1)} collective-permute-done((bf16[3,272,1792]{2,1,0:T(8,128)(2,1)}, bf16[3,272,1792]{2,1,0:T(8,128)(2,1)}, u32[]{:S(2)}, u32[]{:S(2)}) %collective-permute-start) | collective-permute-done | bytes 2924576 | tf_op jit(solution)/shard_map/ppermute | solution.py:18
  99.1 4.4 %fusion.1 = f32[3,272,1792]{2,1,0:T(8,128)S(1)} fusion(bf16[3,272,1792]{2,1,0:T(8,128)(2,1)} %collective-permute-done, pred[272]{0:T(512)(128)(4,1)S(1)} %iota_compare_fusion, pred[]{:T(512)S(6)} %eq.6, f32[3,2,272,1792]{3,2,1,0:T(8,128)} %param.10), kind=kLoop, calls=%fused_computation.6 | loop fusion | flops 4386816 | bytes 14622993 | tf_op jit(solution)/shard_map/jit(_where)/select_n | solution.py:65
  103.6 2.5 copy-done.3
  106.1 0.1 dynamic-slice_convert_fusion
  106.2 3.6 %collective-permute-start.1 = (bf16[3,16,1792]{2,1,0:T(8,128)(2,1)S(1)}, bf16[3,16,1792]{2,1,0:T(8,128)(2,1)S(1)}, u32[]{:S(2)}, u32[]{:S(2)}) collective-permute-start(bf16[3,16,1792]{2,1,0:T(8,128)(2,1)S(1)} %get-tuple-element.7), channel_id=1, source_target_pairs={{0,1},{1,2},{2,3},{3,4},{4,5},{5,6},{6,7},{7,8},{8,9},{9,10},{10,1... | collective-permute-start | bytes 516104 | tf_op jit(solution)/shard_map/ppermute | solution.py:28
  109.8 1.5 collective-permute-start.2
  113.8 2.5 collective-permute-done.1
  116.2 4.2 %collective-permute-done.2 = bf16[3,16,1792]{2,1,0:T(8,128)(2,1)S(1)} collective-permute-done((bf16[3,16,1792]{2,1,0:T(8,128)(2,1)S(1)}, bf16[3,16,1792]{2,1,0:T(8,128)(2,1)S(1)}, u32[]{:S(2)}, u32[]{:S(2)}) %collective-permute-start.2) | collective-permute-done | bytes 172064 | tf_op jit(solution)/shard_map/ppermute | solution.py:29
  120.4 0.1 fusion.10
  120.5 6.3 %dynamic_update_slice.9 = f32[3,608,1792]{2,1,0:T(8,128)} pad(f32[3,16,1792]{2,1,0:T(8,128)S(1)} %get-tuple-element.10, f32[]{:T(128)} %constant.130.clone.1), padding=0_0x0_592x0_0 | pad | bytes 13418500 | tf_op jit(solution)/shard_map/dynamic_update_slice | solution.py:76
  126.8 2.9 constant_dynamic-update-slice_fusion
  129.8 2.0 dynamic_update_slice.11
  131.7 4.0 %dynamic-slice_select_fusion = f32[3,304,1792]{2,1,0:T(8,128)S(1)} fusion(f32[3,608,1792]{2,1,0:T(8,128)} %dynamic_update_slice.11, s32[]{:T(128)S(6)} %select_n.94, pred[304]{0:T(512)(128)(4,1)S(1)} %iota_compare_fusion.1), kind=kLoop, calls=%fused_computation.3 | loop fusion | flops 1634304 | bytes 13074740 | tf_op jit(solution)/shard_map/jit(_where)/select_n | solution.py:81
  135.8 2.8 copy-done.2
  138.5 1.1 fusion.7
  139.6 41.3 %reduce-scatter.2.cloned.1.call-done = bf16[304,1792]{1,0:T(8,128)(2,1)} async-done(((bf16[4864,1792]{1,0:T(8,128)(2,1)}), bf16[304,1792]{1,0:T(8,128)(2,1)}) %reduce-scatter.2.cloned.1.call-update) | async-done | bytes 1089552 | tf_op jit(solution)/shard_map/reduce_scatter | solution.py:87
  180.9 4.9 %subtract_bitcast_fusion = (f32[1,304,1792]{2,1,0:T(8,128)S(1)}, f32[1,304,1792]{2,1,0:T(8,128)S(1)}, f32[1,304,1792]{2,1,0:T(8,128)S(1)}) fusion(f32[3,304,1792]{2,1,0:T(8,128)} %copy-done.2, bf16[304,1792]{1,0:T(8,128)(2,1)} %reduce-scatter.2.cloned.1.call-done), kind=kLoop, calls=%fused_computation.20 | loop fusion | flops 8716288 | bytes 14163968 | tf_op jit(solution)/shard_map/stack | solution.py:103
  185.8 3.2 %pad_maximum_fusion = f32[3,304,1792]{2,1,0:T(8,128)} fusion(f32[1,304,1792]{2,1,0:T(8,128)S(1)} %get-tuple-element.5, f32[1,304,1792]{2,1,0:T(8,128)S(1)} %get-tuple-element.6, f32[1,304,1792]{2,1,0:T(8,128)S(1)} %get-tuple-element.4), kind=kLoop, calls=%fused_computation.2 | loop fusion | flops 3268608 | bytes 13074432 | tf_op jit(solution)/shard_map/stack | solution.py:103
  189.0 108.9 %all-gather.2.cloned.1.call-done = bf16[4864,1792]{1,0:T(8,128)(2,1)} async-done(((bf16[304,1792]{1,0:T(8,128)(2,1)}), bf16[4864,1792]{1,0:T(8,128)(2,1)}) %all-gather.2.cloned.1.call-update) | async-done | bytes 17432592 | tf_op jit(solution)/shard_map/all_gather | solution.py:82
  298.0 12.8 %convolution_convert_fusion.1 = bf16[256,1792]{1,0:T(8,128)(2,1)} fusion(bf16[4864,1792]{1,0:T(8,128)(2,1)} %all-gather.2.cloned.1.call-done, bf16[4864,256]{1,0:T(8,128)(2,1)S(1)} %copy-done.4, pred[4864]{0:T(1024)(128)(4,1)S(1)} %get-tuple-element.35, pred[4864]{0:T(1024)(128)(4,1)S(1)} %get-tuple-element.34), kind=kOutput, calls=%fused_computation.11 | convolution fusion | flops 4465688576 | bytes 20850176 | tf_op jit(solution)/shard_map/dot_general | solution.py:84
  (21 shorter events, 0.1 us)
Async XLA Ops:
  7.2 40.9 %copy-start = (bf16[256,1792]{1,0:T(8,128)(2,1)S(1)}, bf16[256,1792]{1,0:T(8,128)(2,1)}, u32[]{:S(2)}) copy-start(bf16[256,1792]{1,0:T(8,128)(2,1)} %param.15) | copy-start | bytes 2752516
  7.2 173.8 %reduce-scatter.2.cloned.1.call-start = ((), (), s32[]{:S(2)}) async-start(), calls=%async_computation.1 | async-start | bytes 18522112 | tf_op jit(solution)/shard_map/reduce_scatter | solution.py:87
  59.8 7.2 %copy-start.5 = (s32[16]{0:T(128)S(1)}, s32[16]{0:T(128)}, u32[]{:S(2)}) copy-start(s32[16]{0:T(128)} %param.13) | copy-start | bytes 196
  59.8 238.2 %all-gather.2.cloned.1.call-start = ((), (), s32[]{:S(2)}) async-start(), calls=%async_computation.2 | async-start | bytes 18522112 | tf_op jit(solution)/shard_map/all_gather | solution.py:82
  64.4 34.8 %collective-permute-start = (bf16[3,272,1792]{2,1,0:T(8,128)(2,1)}, bf16[3,272,1792]{2,1,0:T(8,128)(2,1)}, u32[]{:S(2)}, u32[]{:S(2)}) collective-permute-start(bf16[3,272,1792]{2,1,0:T(8,128)(2,1)} %fusion.2), channel_id=1, source_target_pairs={{0,16},{16,32},{32,48},{48,64},{64,80},{80,96},{96,112},{112,0},{1... | collective-permute-start | bytes 8773640 | tf_op jit(solution)/shard_map/ppermute | solution.py:18
  103.5 2.6 copy-start.3
  106.2 10.1 %collective-permute-start.1 = (bf16[3,16,1792]{2,1,0:T(8,128)(2,1)S(1)}, bf16[3,16,1792]{2,1,0:T(8,128)(2,1)S(1)}, u32[]{:S(2)}, u32[]{:S(2)}) collective-permute-start(bf16[3,16,1792]{2,1,0:T(8,128)(2,1)S(1)} %get-tuple-element.7), channel_id=1, source_target_pairs={{0,1},{1,2},{2,3},{3,4},{4,5},{5,6},{6,7},{7,8},{8,9},{9,10},{10,1... | collective-permute-start | bytes 516104 | tf_op jit(solution)/shard_map/ppermute | solution.py:28
  109.8 10.7 %collective-permute-start.2 = (bf16[3,16,1792]{2,1,0:T(8,128)(2,1)S(1)}, bf16[3,16,1792]{2,1,0:T(8,128)(2,1)S(1)}, u32[]{:S(2)}, u32[]{:S(2)}) collective-permute-start(bf16[3,16,1792]{2,1,0:T(8,128)(2,1)S(1)} %get-tuple-element.8), channel_id=1, source_target_pairs={{1,0},{2,1},{3,2},{4,3},{5,4},{6,5},{7,6},{8,7},{9,8},{10,9},{11,1... | collective-permute-start | bytes 516104 | tf_op jit(solution)/shard_map/ppermute | solution.py:29
  120.4 6.4 %slice-start = ((s8[5849088]{0:T(1024)(128)(4,1)}), s8[4194304]{0:T(1024)(128)(4,1)S(1)}, s32[]{:S(2)}) async-start(s8[5849088]{0:T(1024)(128)(4,1)} %bitcast.83), calls=%async_computation.3 | async-start | bytes 8388608
  120.5 6.3 %slice-start.1 = ((s8[5849088]{0:T(1024)(128)(4,1)}), s8[1654784]{0:T(1024)(128)(4,1)S(1)}, s32[]{:S(2)}) async-start(s8[5849088]{0:T(1024)(128)(4,1)} %bitcast.83), calls=%async_computation.4 | async-start | bytes 3309568
  135.8 2.8 copy-start.2
  185.8 112.1 %copy-start.4 = (bf16[4864,256]{1,0:T(8,128)(2,1)S(1)}, bf16[4864,256]{1,0:T(8,128)(2,1)}, u32[]{:S(2)}) copy-start(bf16[4864,256]{1,0:T(8,128)(2,1)} %gather_fusion) | copy-start | bytes 7471108
  298.0 12.8 %copy-start.1 = (bf16[256,1792]{1,0:T(8,128)(2,1)S(1)}, bf16[256,1792]{1,0:T(8,128)(2,1)}, u32[]{:S(2)}) copy-start(bf16[256,1792]{1,0:T(8,128)(2,1)} %param.15) | copy-start | bytes 2752516
Sparse Core Ops, SparseCore 0:
  59.9 121.0 reduce-scatter.1
  183.4 114.5 all-gather.1
where the time goes:
time: 318 us
  waiting for transfers between devices  185 us (58%)
  local copies, waits for them, and re-layouts  43.4 us (14%)
  other arithmetic  38.2 us (12%)
  matrix products  24.5 us (8%)
  between operations  18.6 us (6%)
  starting transfers between devices  7.73 us (2%)
    all_gather x1, waiting for transfers between devices, body(): lax.all_gather(moved[0].astype(jnp.bfloat16), 'fsdp', axis=0, tiled=True)  109 us
    reduce_scatter x1, waiting for transfers between devices, body(): lax.psum_scatter(lax.dot_general(picked, cotangent, (((0,), (0,)), ((), (...  41.3 us
    ppermute x1, waiting for transfers between devices, passed_along(): return lax.ppermute(value, axis, pairs)  28.2 us
    gather x1, local copies, waits for them, and re-layouts, pick_columns(): picked = jnp.take(tokens, target, axis=1)  14.4 us
    dot_general x1, matrix products, body(): hidden = jnp.dot(picked, block_rows, preferred_element_type=jnp.float32)  12.8 us
    dot_general x1, matrix products, body(): lax.dot_general(picked, cotangent, (((0,), (0,)), ((), ())), preferred_el...  11.7 us
    lt x1, other arithmetic, pick_columns(): offsets < length  10.8 us
    select_n x1, other arithmetic, pick_columns(): picked = jnp.take(tokens, target, axis=1)  10.8 us
  transfers between devices with their start and end apart: 5, of which 5 were waited for; matrix products, arithmetic and copies ran while one was open for 11% of the time, Pallas kernels for 0%

commit v1 on v0

--- a/solution.py
+++ b/solution.py
@@ -79,7 +79,12 @@
     moved = lax.dynamic_slice_in_dim(extended, new_start - old_start + margin, cap_new, 1)
     slot_new = jnp.arange(cap_new, dtype=jnp.int32)
     moved = jnp.where((slot_new < new_len)[None, :, None], moved, jnp.zeros((), jnp.float32))
-    block_rows = lax.all_gather(moved[0].astype(jnp.bfloat16), "fsdp", axis=0, tiled=True)
+    block_rows = jnp.concatenate(
+        lax.all_to_all(
+            jnp.stack([moved[0].astype(jnp.bfloat16)] * lax.axis_size("fsdp")), "fsdp", 0, 0
+        ),
+        axis=0,
+    )
     picked = pick_columns(tokens, own_new, block_rows.shape[0], cap_new)
     hidden = jnp.dot(picked, block_rows, preferred_element_type=jnp.float32)
     activations = hidden.astype(jnp.bfloat16)

time: 318 us -> 380 us (1.19); the launches traced: 318 us -> 375 us
  blocking collectives: 0 us -> 214 us
  waiting for transfers between devices: 185 us -> 35.1 us
  matrix products: 24.5 us -> 17.6 us
    all_to_all x0 -> x1, blocking collectives: none -> 214 us  [body(): lax.all_to_all(jnp.stack([moved[0].astype(jnp.bfloat16)] * lax.axis_size(...]
    all_gather x1 -> x0, waiting for transfers between devices: 109 us -> none  [body(): lax.all_gather(moved[0].astype(jnp.bfloat16), 'fsdp', axis=0, tiled=True)]
    reduce_scatter x1, waiting for transfers between devices: 41.3 us -> 0.01 us  [body(): lax.psum_scatter(lax.dot_general(picked, cotangent, (((0,), (0,)), ((), (...]
    dot_general x1, matrix products: 12.8 us -> 5.94 us  [body(): hidden = jnp.dot(picked, block_rows, preferred_element_type=jnp.float32)]
  transfers between devices with their start and end apart: 5 -> 4, of which waited for: 5 -> 3; matrix products, arithmetic and copies ran while one was open for 11% -> 9% of each run, Pallas kernels for 0% -> 0%
where the time goes in v1:
time: 380 us; the launch traced here: 375 us
  blocking collectives  214 us (56%)
  local copies, waits for them, and re-layouts  43.9 us (12%)
  other arithmetic  38.3 us (10%)
  waiting for transfers between devices  35.1 us (9%)
  between operations  18.6 us (5%)
  matrix products  17.6 us (5%)
  starting transfers between devices  7.53 us (2%)
    all_to_all x1, blocking collectives, body(): lax.all_to_all(jnp.stack([moved[0].astype(jnp.bfloat16)] * lax.axis_size(...  214 us
    ppermute x1, waiting for transfers between devices, passed_along(): return lax.ppermute(value, axis, pairs)  28.2 us
    gather x1, local copies, waits for them, and re-layouts, pick_columns(): picked = jnp.take(tokens, target, axis=1)  14.4 us
    dot_general x1, matrix products, body(): lax.dot_general(picked, cotangent, (((0,), (0,)), ((), ())), preferred_el...  11.7 us
    lt x1, other arithmetic, pick_columns(): offsets < length  10.9 us
    select_n x1, other arithmetic, pick_columns(): picked = jnp.take(tokens, target, axis=1)  10.8 us
    unnamed x17, local copies, waits for them, and re-layouts  8.65 us
    another operation x2, other arithmetic, body(): return (jnp.stack([new_weight, moment_one, moment_two]), activations)  8.08 us
  transfers between devices with their start and end apart: 4, of which 3 were waited for; matrix products, arithmetic and copies ran while one was open for 9% of the time, Pallas kernels for 0%

profile of v1, /device:TPU:1, one launch (start us, length us, event | category | flops | bytes accessed | tf_op | source)
XLA Modules:
  0.0 375.2 jit_solution(1636071945300808369)
XLA Ops:
  7.2 0.0 reduce-scatter.2.cloned.1.call-start
  7.2 0.8 fusion.20
  8.0 0.7 fusion.23
  8.7 10.9 %fusion.15 = (pred[4864]{0:T(1024)(128)(4,1)S(1)}, pred[4864]{0:T(1024)(128)(4,1)S(1)}) fusion(s32[]{:T(128)} %bitcast.26, s32[]{:T(128)} %bitcast.25, s32[]{:T(128)} %bitcast.24, s32[]{:T(128)} %bitcast.23, s32[]{:T(128)} %bitcast.22, s32[]{:T(128)} %bitcast.21, s32[]{:T(128)} %bitcast.20, s32[]{:T(128)} %bitcast.19, s32[]{:T(128)} %bitcast.18, ...), kind=kLoop, calls=%fused_computation.46 | loop fusion | flops 491264 | bytes 9796 | tf_op jit(solution)/shard_map/lt | solution.py:42
  19.6 10.8 %compare_select_fusion = s32[4864]{0:T(1024)S(1)} fusion(s32[]{:T(128)} %bitcast.26, s32[]{:T(128)} %bitcast.25, s32[]{:T(128)} %bitcast.24, s32[]{:T(128)} %bitcast.23, s32[]{:T(128)} %bitcast.22, s32[]{:T(128)} %bitcast.21, s32[]{:T(128)} %bitcast.20, s32[]{:T(128)} %bitcast.19, s32[]{:T(128)} %bitcast.18, s32[]{:T(128)} %bitcast.17, s32[]{:T(128)} %bitcast.16, ...), kind=kLoop, calls=%fused_computation.35 | loop fusion | flops 272384 | bytes 19524 | tf_op jit(solution)/shard_map/jit(_take)/jit(_where)/select_n | solution.py:41
  30.5 3.3 copy.10
  33.7 14.4 %gather_fusion = bf16[4864,256]{1,0:T(8,128)(2,1)} fusion(bf16[256,4096]{0,1:T(8,128)(2,1)S(1)} %copy.10, s32[5120]{0:T(1024)S(1)} %pad_clamp_fusion), kind=kCustom, calls=%fused_computation.clone | custom fusion | bytes 5000192 | tf_op jit(solution)/shard_map/jit(_take)/gather | solution.py:41
  48.1 11.7 %convolution_convert_fusion = bf16[4864,1792]{1,0:T(8,128)(2,1)} fusion(bf16[256,1792]{1,0:T(8,128)(2,1)S(1)} %copy-done, bf16[4864,256]{1,0:T(8,128)(2,1)} %gather_fusion, pred[4864]{0:T(1024)(128)(4,1)S(1)} %get-tuple-element.35, pred[4864]{0:T(1024)(128)(4,1)S(1)} %get-tuple-element.34), kind=kOutput, calls=%fused_computation.1 | convolution fusion | flops 4473946112 | bytes 20850176 | tf_op jit(solution)/shard_map/dot_general | solution.py:93
  59.8 4.5 %fusion.2 = bf16[3,272,1792]{2,1,0:T(8,128)(2,1)} fusion(f32[3,2,272,1792]{3,2,1,0:T(8,128)} %param.10), kind=kLoop, calls=%fused_computation.9 | loop fusion | bytes 5849088 | tf_op jit(solution)/shard_map/convert_element_type | solution.py:62
  64.4 2.6 collective-permute-start
  67.0 0.6 dynamic_slice.29
  68.2 1.4 fusion.21
  70.9 28.2 %collective-permute-done = bf16[3,272,1792]{2,1,0:T(8,128)(2,1)} collective-permute-done((bf16[3,272,1792]{2,1,0:T(8,128)(2,1)}, bf16[3,272,1792]{2,1,0:T(8,128)(2,1)}, u32[]{:S(2)}, u32[]{:S(2)}) %collective-permute-start) | collective-permute-done | bytes 2924576 | tf_op jit(solution)/shard_map/ppermute | solution.py:18
  99.1 4.4 %fusion.1 = f32[3,272,1792]{2,1,0:T(8,128)S(1)} fusion(bf16[3,272,1792]{2,1,0:T(8,128)(2,1)} %collective-permute-done, pred[272]{0:T(512)(128)(4,1)S(1)} %iota_compare_fusion, pred[]{:T(512)S(6)} %eq.6, f32[3,2,272,1792]{3,2,1,0:T(8,128)} %param.10), kind=kLoop, calls=%fused_computation.6 | loop fusion | flops 4386816 | bytes 14622993 | tf_op jit(solution)/shard_map/jit(_where)/select_n | solution.py:65
  103.5 2.5 copy-done.3
  106.1 0.1 dynamic-slice_convert_fusion
  106.1 3.6 collective-permute-start.1
  109.8 1.3 collective-permute-start.2
  113.6 2.6 collective-permute-done.1
  116.2 4.2 %collective-permute-done.2 = bf16[3,16,1792]{2,1,0:T(8,128)(2,1)S(1)} collective-permute-done((bf16[3,16,1792]{2,1,0:T(8,128)(2,1)S(1)}, bf16[3,16,1792]{2,1,0:T(8,128)(2,1)S(1)}, u32[]{:S(2)}, u32[]{:S(2)}) %collective-permute-start.2) | collective-permute-done | bytes 172064 | tf_op jit(solution)/shard_map/ppermute | solution.py:29
  120.5 0.1 fusion.13
  120.5 6.3 %dynamic_update_slice.9 = f32[3,608,1792]{2,1,0:T(8,128)} pad(f32[3,16,1792]{2,1,0:T(8,128)S(1)} %get-tuple-element.10, f32[]{:T(128)} %constant.130.clone.1), padding=0_0x0_592x0_0 | pad | bytes 13418500 | tf_op jit(solution)/shard_map/dynamic_update_slice | solution.py:76
  126.9 2.9 constant_dynamic-update-slice_fusion
  129.8 1.9 dynamic_update_slice.11
  131.7 4.0 %dynamic-slice_select_fusion = f32[3,304,1792]{2,1,0:T(8,128)S(1)} fusion(f32[3,608,1792]{2,1,0:T(8,128)} %dynamic_update_slice.11, s32[]{:T(128)S(6)} %select_n.94, pred[304]{0:T(512)(128)(4,1)S(1)} %iota_compare_fusion.1), kind=kLoop, calls=%fused_computation.3 | loop fusion | flops 1634304 | bytes 13074740 | tf_op jit(solution)/shard_map/jit(_where)/select_n | solution.py:81
  135.8 2.8 copy-done.2
  138.5 0.1 fusion.11
  138.7 1.5 stack.17
  140.2 214.2 %all_to_all.5 = bf16[16,304,1792]{2,1,0:T(8,128)(2,1)S(1)} all-to-all(bf16[16,304,1792]{2,1,0:T(8,128)(2,1)S(1)} %stack.17), channel_id=1, replica_groups=mesh['dp'=8,'fsdp'=16] {'fsdp'}, dimensions={0} | all-to-all | bytes 34865152 | tf_op jit(solution)/shard_map/all_to_all | solution.py:83
  354.3 5.9 %convolution_convert_fusion.1 = bf16[256,1792]{1,0:T(8,128)(2,1)} fusion(bf16[4864,1792]{1,0:T(8,128)(2,1)S(1)} %bitcast.93, bf16[4864,256]{1,0:T(8,128)(2,1)S(1)} %copy-done.4, pred[4864]{0:T(1024)(128)(4,1)S(1)} %get-tuple-element.35, pred[4864]{0:T(1024)(128)(4,1)S(1)} %get-tuple-element.34), kind=kOutput, calls=%fused_computation.11 | convolution fusion | flops 4465688576 | bytes 20850176 | tf_op jit(solution)/shard_map/dot_general | solution.py:89
  360.3 4.9 %fusion.9 = (f32[1,304,1792]{2,1,0:T(8,128)S(1)}, f32[1,304,1792]{2,1,0:T(8,128)S(1)}, f32[1,304,1792]{2,1,0:T(8,128)S(1)}) fusion(f32[3,304,1792]{2,1,0:T(8,128)} %copy-done.2, bf16[304,1792]{1,0:T(8,128)(2,1)} %reduce-scatter.2.cloned.1.call-done), kind=kLoop, calls=%fused_computation.23 | loop fusion | flops 8716288 | bytes 14163968 | tf_op jit(solution)/shard_map/stack | solution.py:108
  365.2 3.2 pad_maximum_fusion
  (20 shorter events, 0.1 us)
Async XLA Ops:
  7.2 41.0 %copy-start = (bf16[256,1792]{1,0:T(8,128)(2,1)S(1)}, bf16[256,1792]{1,0:T(8,128)(2,1)}, u32[]{:S(2)}) copy-start(bf16[256,1792]{1,0:T(8,128)(2,1)} %param.15) | copy-start | bytes 2752516
  7.2 353.1 %reduce-scatter.2.cloned.1.call-start = ((), (), s32[]{:S(2)}) async-start(), calls=%async_computation.2 | async-start | bytes 18522112 | tf_op jit(solution)/shard_map/reduce_scatter | solution.py:92
  59.8 7.2 %copy-start.5 = (s32[16]{0:T(128)S(1)}, s32[16]{0:T(128)}, u32[]{:S(2)}) copy-start(s32[16]{0:T(128)} %param.13) | copy-start | bytes 196
  64.4 34.8 %collective-permute-start = (bf16[3,272,1792]{2,1,0:T(8,128)(2,1)}, bf16[3,272,1792]{2,1,0:T(8,128)(2,1)}, u32[]{:S(2)}, u32[]{:S(2)}) collective-permute-start(bf16[3,272,1792]{2,1,0:T(8,128)(2,1)} %fusion.2), channel_id=1, source_target_pairs={{0,16},{16,32},{32,48},{48,64},{64,80},{80,96},{96,112},{112,0},{1... | collective-permute-start | bytes 8773640 | tf_op jit(solution)/shard_map/ppermute | solution.py:18
  103.5 2.6 copy-start.3
  106.1 10.1 %collective-permute-start.1 = (bf16[3,16,1792]{2,1,0:T(8,128)(2,1)S(1)}, bf16[3,16,1792]{2,1,0:T(8,128)(2,1)S(1)}, u32[]{:S(2)}, u32[]{:S(2)}) collective-permute-start(bf16[3,16,1792]{2,1,0:T(8,128)(2,1)S(1)} %get-tuple-element.7), channel_id=1, source_target_pairs={{0,1},{1,2},{2,3},{3,4},{4,5},{5,6},{6,7},{7,8},{8,9},{9,10},{10,1... | collective-permute-start | bytes 516104 | tf_op jit(solution)/shard_map/ppermute | solution.py:28
  109.8 10.7 %collective-permute-start.2 = (bf16[3,16,1792]{2,1,0:T(8,128)(2,1)S(1)}, bf16[3,16,1792]{2,1,0:T(8,128)(2,1)S(1)}, u32[]{:S(2)}, u32[]{:S(2)}) collective-permute-start(bf16[3,16,1792]{2,1,0:T(8,128)(2,1)S(1)} %get-tuple-element.8), channel_id=1, source_target_pairs={{1,0},{2,1},{3,2},{4,3},{5,4},{6,5},{7,6},{8,7},{9,8},{10,9},{11,1... | collective-permute-start | bytes 516104 | tf_op jit(solution)/shard_map/ppermute | solution.py:29
  120.5 6.4 %slice-start = ((s8[5849088]{0:T(1024)(128)(4,1)}), s8[4194304]{0:T(1024)(128)(4,1)S(1)}, s32[]{:S(2)}) async-start(s8[5849088]{0:T(1024)(128)(4,1)} %bitcast.91), calls=%async_computation.3 | async-start | bytes 8388608
  120.5 6.3 %slice-start.1 = ((s8[5849088]{0:T(1024)(128)(4,1)}), s8[1654784]{0:T(1024)(128)(4,1)S(1)}, s32[]{:S(2)}) async-start(s8[5849088]{0:T(1024)(128)(4,1)} %bitcast.91), calls=%async_computation.4 | async-start | bytes 3309568
  135.8 2.8 copy-start.2
  140.1 214.2 %copy-start.4 = (bf16[4864,256]{1,0:T(8,128)(2,1)S(1)}, bf16[4864,256]{1,0:T(8,128)(2,1)}, u32[]{:S(2)}) copy-start(bf16[4864,256]{1,0:T(8,128)(2,1)} %gather_fusion) | copy-start | bytes 7471108
  365.1 3.2 copy-start.1
Sparse Core Ops, SparseCore 0:
  59.9 264.5 reduce-scatter.1
